TPU v7x, 32 devices: a whole 2x2x4 slice. The times are simulated.
32 devices in a mesh: shot: 8 (over z, y), off: 4 (over x, core).
Axes of the slice: x: 2, y: 2, z: 4, core: 2. Of those that a mesh axis runs over, the one named last changes fastest.
Arguments:
- traces: bfloat16 [32, 768, 2048], P('shot', 'off'), may hold values from -60 to 60
- offset_bin: int32 [32, 768], P('shot', 'off'), may hold values from 0 to 31, as said below
- rec_id: int32 [32, 768], P('shot', 'off'), may hold values from 0 to 2047, as said below
- cmp_id: int32 [32, 768], P('shot', 'off'), may hold values from 0 to 4095, as said below
- rec_owner: int32 [2048], replicated, may hold values from 0 to 7, as said below
- rec_slot: int32 [2048], replicated, may hold values from 0 to 255
- cmp_owner: int32 [4096], replicated, may hold values from 0 to 7, as said below
- cmp_slot: int32 [4096], replicated, may hold values from 0 to 511
Outputs:
- source_term: float32 [32, 640], P('shot')
- offset_term: float32 [32, 640], P('off')
- receiver_term: float32 [2048, 640], P(('shot', 'off'))
- midpoint_term: float32 [4096, 640], P(('shot', 'off'))
Inputs may be any that keep to these rules, and one draw needn't show every extreme that they name: `offset_bin`: a trace at position j of its shot has a bin of (j // 192) * 8 to (j // 192 + 1) * 8 - 1. rec_owner[r] * 256 + rec_slot[r] takes every value below 2048 exactly once. cmp_owner[c] * 512 + cmp_slot[c] takes every value below 4096 exactly once. `rec_id`: of the traces of one device's block (4 shots by 192 traces) at most 192 have receivers of any one owner; for every offset group some owner gets exactly 192 from every block of that group. `cmp_id`: of the traces of one device's block at most 192 have midpoints of any one owner; for every offset group some owner gets exactly 192 from every block of that group.
All inputs are finite; a program needn't handle non-finite values.
Results may differ from a plain program's by a relative error of at most 0.0035.
Values may be sent and summed in bfloat16 or wider, within the bound.
A program may use at most 64 MiB of HBM per device.

v0:
```python
import math

import jax
import jax.numpy as jnp
from jax import lax
from jax.sharding import PartitionSpec as P

NF = 640
OFFB_DEV = 8
SWEEPS = 2


OMEGA = 0.35
FLOOR = 0.05


def spectral_table(samples, freqs):
    sample_idx = jnp.arange(samples, dtype=jnp.int32)
    freq_idx = jnp.arange(freqs, dtype=jnp.int32)
    phases = sample_idx[:, None] * freq_idx[None, :] % samples
    angles = phases.astype(jnp.float32) * (2.0 * math.pi / samples)
    tapers = 0.5 - 0.5 * jnp.cos((sample_idx.astype(jnp.float32) + 0.5) * (2.0 * math.pi / samples))
    weights = (tapers * math.sqrt(8.0 / (3.0 * samples)))[:, None]
    return jnp.concatenate([weights * jnp.cos(angles), -weights * jnp.sin(angles)], axis=1).astype(
        jnp.bfloat16
    )


def log_spectrum(trace_rows, table, freqs):
    products = jnp.dot(trace_rows, table, preferred_element_type=jnp.float32)
    real_part = products[:, :freqs]
    imag_part = products[:, freqs:]
    return jnp.log(real_part * real_part + imag_part * imag_part + FLOOR)


def route_rows(identity, owner_table, slot_table, n_shot, capacity):
    tr_dev = identity.shape[0]
    owner_of = owner_table[identity]
    slot_of = slot_table[identity]
    owner_hot = (owner_of[:, None] == jnp.arange(n_shot, dtype=jnp.int32)[None, :]).astype(
        jnp.int32
    )
    rank_in = jnp.sum(jnp.cumsum(owner_hot, axis=0) * owner_hot, axis=1) - 1
    position = owner_of * capacity + rank_in
    sources = (
        jnp.full((n_shot * capacity,), tr_dev, jnp.int32)
        .at[position]
        .set(jnp.arange(tr_dev, dtype=jnp.int32))
    )
    sent_slot = jnp.concatenate([slot_of, jnp.full((1,), -1, jnp.int32)])[sources]
    return (position, sources, sent_slot)


def owner_totals(rows, slot_ids, count):
    member = slot_ids[None, :] == jnp.arange(count, dtype=jnp.int32)[:, None]
    totals = jnp.dot(member.astype(jnp.bfloat16), rows, preferred_element_type=jnp.float32)
    return (totals, jnp.sum(member.astype(jnp.float32), axis=1))


def values_for(values, slot_ids, n_shot, capacity):
    safe_slot = jnp.maximum(slot_ids, 0)
    picked = jnp.where(
        (slot_ids >= 0)[:, None], values[safe_slot], jnp.zeros((1, NF), jnp.bfloat16)
    )
    return picked.reshape(n_shot, capacity, NF)


def shards(traces, offset_bin, rec_id, cmp_id, rec_owner, rec_slot, cmp_owner, cmp_slot):
    shot_dev, tr_off, samples = traces.shape
    n_shot = lax.axis_size("shot")
    n_off = lax.axis_size("off")
    tr_dev = shot_dev * tr_off
    capacity = 2 * tr_dev // n_shot
    rec_dev = rec_owner.shape[0] // n_shot
    cmp_dev = cmp_owner.shape[0] // n_shot
    table = spectral_table(samples, NF)
    logs = log_spectrum(traces.reshape(tr_dev, samples), table, NF)
    local_bins = offset_bin.reshape(tr_dev) - lax.axis_index("off") * OFFB_DEV
    bin_hot = (local_bins[:, None] == jnp.arange(OFFB_DEV, dtype=jnp.int32)[None, :]).astype(
        jnp.float32
    )
    bin_count = jnp.sum(bin_hot, axis=0)
    rec_place, rec_source, rec_sent = route_rows(
        rec_id.reshape(tr_dev), rec_owner, rec_slot, n_shot, capacity
    )
    cmp_place, cmp_source, cmp_sent = route_rows(
        cmp_id.reshape(tr_dev), cmp_owner, cmp_slot, n_shot, capacity
    )
    rec_rows_held = rec_dev // n_off
    cmp_rows_held = cmp_dev // n_off
    source_term = jnp.zeros((shot_dev, NF), jnp.float32)
    offset_term = jnp.zeros((OFFB_DEV, NF), jnp.float32)
    rec_term = jnp.zeros((rec_rows_held, NF), jnp.float32)
    cmp_term = jnp.zeros((cmp_rows_held, NF), jnp.float32)
    rec_trace = jnp.zeros((tr_dev, NF), jnp.float32)
    cmp_trace = jnp.zeros((tr_dev, NF), jnp.float32)
    zero_row = jnp.zeros((1, NF), jnp.bfloat16)
    for sweep_no in range(SWEEPS):
        per_shot = (logs.reshape(shot_dev, tr_off, NF) - source_term[:, None, :]).reshape(
            tr_dev, NF
        )
        offset_part = jnp.dot(
            bin_hot,
            offset_term,
            precision=lax.Precision.HIGHEST,
            preferred_element_type=jnp.float32,
        )
        residual = per_shot - offset_part - rec_trace - cmp_trace
        rounded = jnp.concatenate([residual.astype(jnp.bfloat16), zero_row], axis=0)
        rec_rows = rounded[rec_source].reshape(n_shot, capacity, NF)
        cmp_rows = rounded[cmp_source].reshape(n_shot, capacity, NF)
        received = (
            lax.all_to_all(rec_rows, "shot", split_axis=0, concat_axis=0, tiled=True),
            lax.all_to_all(
                rec_sent.reshape(n_shot, capacity), "shot", split_axis=0, concat_axis=0, tiled=True
            ),
            lax.all_to_all(cmp_rows, "shot", split_axis=0, concat_axis=0, tiled=True),
            lax.all_to_all(
                cmp_sent.reshape(n_shot, capacity), "shot", split_axis=0, concat_axis=0, tiled=True
            ),
        )
        shot_sums = jnp.sum(residual.reshape(shot_dev, tr_off, NF), axis=1)
        bin_sums = jnp.dot(
            bin_hot.T, residual, precision=lax.Precision.HIGHEST, preferred_element_type=jnp.float32
        )
        bin_total, bin_number = lax.psum((bin_sums, bin_count), "shot")
        offset_term = offset_term + OMEGA * bin_total / (bin_number[:, None] + 1.0)
        rec_ids_in = received[1].reshape(-1)
        cmp_ids_in = received[3].reshape(-1)
        rec_sums, rec_number = owner_totals(received[0].reshape(-1, NF), rec_ids_in, rec_dev)
        cmp_sums, cmp_number = owner_totals(received[2].reshape(-1, NF), cmp_ids_in, cmp_dev)
        last_sweep = sweep_no + 1 == SWEEPS
        shot_total = lax.psum(shot_sums, "off")
        rec_total, rec_all, cmp_total, cmp_all = (
            lax.psum_scatter(rec_sums, "off", scatter_dimension=0, tiled=True),
            lax.psum_scatter(rec_number, "off", scatter_dimension=0, tiled=True),
            lax.psum_scatter(cmp_sums, "off", scatter_dimension=0, tiled=True),
            lax.psum_scatter(cmp_number, "off", scatter_dimension=0, tiled=True),
        )
        rec_term = rec_term + OMEGA * rec_total / (rec_all[:, None] + 1.0)
        cmp_term = cmp_term + OMEGA * cmp_total / (cmp_all[:, None] + 1.0)
        if not last_sweep:
            rec_values, cmp_values = (
                lax.all_gather(rec_term.astype(jnp.bfloat16), "off", axis=0, tiled=True),
                lax.all_gather(cmp_term.astype(jnp.bfloat16), "off", axis=0, tiled=True),
            )
        source_term = source_term + OMEGA * shot_total / (tr_off * n_off + 1.0)
        if not last_sweep:
            rec_reply = values_for(rec_values, rec_ids_in, n_shot, capacity)
            cmp_reply = values_for(cmp_values, cmp_ids_in, n_shot, capacity)
            returned = (
                lax.all_to_all(rec_reply, "shot", split_axis=0, concat_axis=0, tiled=True),
                lax.all_to_all(cmp_reply, "shot", split_axis=0, concat_axis=0, tiled=True),
            )
            rec_trace = returned[0].reshape(-1, NF)[rec_place].astype(jnp.float32)
            cmp_trace = returned[1].reshape(-1, NF)[cmp_place].astype(jnp.float32)
    return (source_term, offset_term, rec_term, cmp_term)


def solution(mesh):
    return jax.shard_map(
        shards,
        mesh=mesh,
        in_specs=(
            P("shot", "off", None),
            P("shot", "off"),
            P("shot", "off"),
            P("shot", "off"),
            P(),
            P(),
            P(),
            P(),
        ),
        out_specs=(
            P("shot", None),
            P("off", None),
            P(("shot", "off"), None),
            P(("shot", "off"), None),
        ),
        check_vma=False,
    )
```

profile of v0, /device:TPU:0, one launch (start us, length us, event | category | flops | bytes accessed | tf_op | source)
XLA Modules:
  0.0 518.7 jit_solution(7989366931601015454)
XLA Ops:
  28.2 5.9 %gather_fusion.2 = s32[1536]{0:T(1024)S(1)} fusion(s32[769]{0:T(1024)S(1)} %get-tuple-element.14, s32[2048]{0:T(1024)S(1)} %pad_clamp_fusion.3), kind=kCustom, calls=%fused_computation.2 | custom fusion | bytes 18432 | tf_op jit(solution)/shard_map/gather | solution.py:50
  34.7 7.3 %all-to-all-start = ((s32[8,1,192]{2,1,0:T(1,128)}), s32[8,1,192]{2,1,0:T(1,128)S(1)}, u32[]{:S(2)}, u32[]{:S(2)}) async-start(s32[8,1,192]{2,1,0:T(1,128)} %all_to_all.32), calls=%async_computation | async-start | bytes 16384 | tf_op jit(solution)/shard_map/all_to_all | solution.py:114
  53.0 22.1 %multiply_convert_fusion = (bf16[2048,640]{1,0:T(8,128)(2,1)S(1)}, bf16[2048,640]{1,0:T(8,128)(2,1)S(1)}) fusion(f32[2048]{0:T(1024)S(1)} %fusion.44, f32[2048]{0:T(1024)S(1)} %subtract_multiply_fusion), kind=kLoop, calls=%fused_computation.26 | loop fusion | flops 23592960 | bytes 5259264 | tf_op jit(solution)/shard_map/convert.1
  75.1 6.1 %fusion.10 = f32[768,1280]{1,0:T(8,128)} fusion(bf16[768,2048]{1,0:T(8,128)(2,1)S(1)} %bitcast.61, bf16[2048,640]{1,0:T(8,128)(2,1)S(1)} %get-tuple-element.15, bf16[2048,640]{1,0:T(8,128)(2,1)S(1)} %get-tuple-element.16), kind=kOutput, calls=%fused_computation.31 | convolution fusion | flops 4037017600 | bytes 12320768 | tf_op jit(solution)/shard_map/dot_general | solution.py:30
  81.4 5.8 %gather_fusion.8 = s32[1536]{0:T(1024)S(1)} fusion(s32[769]{0:T(1024)S(1)} %get-tuple-element.13, s32[2048]{0:T(1024)S(1)} %pad_clamp_fusion.1), kind=kCustom, calls=%fused_computation.8 | custom fusion | bytes 18432 | tf_op jit(solution)/shard_map/gather | solution.py:50
  87.9 6.0 %all-to-all-start.3 = ((s32[8,1,192]{2,1,0:T(1,128)}), s32[8,1,192]{2,1,0:T(1,128)S(1)}, u32[]{:S(2)}, u32[]{:S(2)}) async-start(s32[8,1,192]{2,1,0:T(1,128)} %all_to_all.36), calls=%async_computation.4 | async-start | bytes 16384 | tf_op jit(solution)/shard_map/all_to_all | solution.py:118
  99.4 7.2 %gather_fusion.3 = bf16[1536,640]{1,0:T(8,128)(2,1)} fusion(bf16[769,640]{1,0:T(8,128)(2,1)} %concatenate.18, s32[2048]{0:T(1024)S(1)} %pad_clamp_fusion.3), kind=kCustom, calls=%fused_computation.3 | custom fusion | bytes 3938304 | tf_op jit(solution)/shard_map/gather | solution.py:110
  106.7 6.0 %all-to-all-start.1 = ((bf16[8,192,640]{2,1,0:T(8,128)(2,1)}), bf16[8,192,640]{2,1,0:T(8,128)(2,1)}, u32[]{:S(2)}, u32[]{:S(2)}) async-start(bf16[8,192,640]{2,1,0:T(8,128)(2,1)} %bitcast.68), calls=%async_computation.1 | async-start | bytes 3932160 | tf_op jit(solution)/shard_map/all_to_all | solution.py:113
  112.7 7.2 %gather_fusion.9 = bf16[1536,640]{1,0:T(8,128)(2,1)} fusion(bf16[769,640]{1,0:T(8,128)(2,1)} %concatenate.18, s32[2048]{0:T(1024)S(1)} %pad_clamp_fusion.1), kind=kCustom, calls=%fused_computation.9 | custom fusion | bytes 3938304 | tf_op jit(solution)/shard_map/gather | solution.py:111
  119.9 37.2 %all-to-all-done.1 = bf16[8,192,640]{2,1,0:T(8,128)(2,1)} async-done(((bf16[8,192,640]{2,1,0:T(8,128)(2,1)}), bf16[8,192,640]{2,1,0:T(8,128)(2,1)}, u32[]{:S(2)}, u32[]{:S(2)}) %all-to-all-start.1) | async-done | bytes 1966112 | tf_op jit(solution)/shard_map/all_to_all | solution.py:113
  168.5 11.5 %all-reduce.5 = (f32[512]{0:T(512)}, f32[256]{0:T(256)S(1)}, f32[4,640]{1,0:T(4,128)S(1)}) all-reduce(f32[512]{0:T(512)S(1)} %convert_reduce_fusion, f32[256]{0:T(256)S(1)} %convert_reduce_fusion.1, f32[4,640]{1,0:T(4,128)S(1)} %reduce_sum.62), channel_id=5, replica_groups=mesh['shot'=8,'off'=4] {'off'}, use_global_device_ids=true, to_apply=%region_18.19.clone | all-reduce | flops 3328 | bytes 26624
  180.2 8.5 %reduce-scatter.5.cloned.1.call-done = f32[64,640]{1,0:T(8,128)} async-done(((f32[256,640]{1,0:T(8,128)}), f32[64,640]{1,0:T(8,128)}) %reduce-scatter.5.cloned.1.call-update) | async-done | bytes 163856 | tf_op jit(solution)/shard_map/reduce_scatter | solution.py:135
  189.7 6.0 %all_gather.6 = bf16[256,640]{1,0:T(8,128)(2,1)S(1)} all-gather(bf16[64,640]{1,0:T(8,128)(2,1)S(1)} %fusion.34), channel_id=1, replica_groups=mesh['shot'=8,'off'=4] {'off'}, dimensions={0}, use_global_device_ids=true | all-gather | bytes 409600 | tf_op jit(solution)/shard_map/all_gather | solution.py:144
  216.5 26.4 %reduce-scatter.7.cloned.1.call-done = f32[128,640]{1,0:T(8,128)} async-done(((f32[512,640]{1,0:T(8,128)}), f32[128,640]{1,0:T(8,128)}) %reduce-scatter.7.cloned.1.call-update) | async-done | bytes 327696 | tf_op jit(solution)/shard_map/reduce_scatter | solution.py:137
  244.0 7.8 %all_gather.7 = bf16[512,640]{1,0:T(8,128)(2,1)} all-gather(bf16[128,640]{1,0:T(8,128)(2,1)S(1)} %fusion.27), channel_id=1, replica_groups=mesh['shot'=8,'off'=4] {'off'}, dimensions={0}, use_global_device_ids=true | all-gather | bytes 819200 | tf_op jit(solution)/shard_map/all_gather | solution.py:145
  251.7 7.1 %gather_fusion.10 = bf16[1536,640]{1,0:T(8,128)(2,1)} fusion(bf16[512,640]{1,0:T(8,128)(2,1)} %all_gather.7, s32[2048]{0:T(1024)S(1)} %pad_clamp_fusion), kind=kCustom, calls=%fused_computation.10 | custom fusion | bytes 3938304 | tf_op jit(solution)/shard_map/gather | solution.py:63
  269.9 66.8 %all-reduce.4 = (f32[8,640]{1,0:T(8,128)S(1)}, f32[8]{0:T(128)S(1)}) all-reduce(f32[8,640]{1,0:T(8,128)S(1)} %fusion.31, f32[8]{0:T(128)S(1)} %convert_reduce_fusion.2), channel_id=1, replica_groups=mesh['shot'=8,'off'=4] {'shot'}, use_global_device_ids=true, to_apply=%region_2.3 | all-reduce | flops 5128 | bytes 41024 | tf_op jit(solution)/shard_map/psum | solution.py:126
  347.6 5.7 %fusion.53 = (bf16[768,640]{1,0:T(8,128)(2,1)S(1)}, f32[768,640]{1,0:T(8,128)}) fusion(bf16[768,640]{1,0:T(8,128)(2,1)} %gather_fusion.11, bf16[768,640]{1,0:T(8,128)(2,1)} %gather_fusion.5, f32[8,640]{1,0:T(8,128)S(1)} %get-tuple-element.4, f32[8]{0:T(128)S(1)} %broadcast_add_fusion, s32[768]{0:T(1024)S(1)} %sub.57, ...), kind=kOutput, calls=%fused_computation.125 | convolution fusion | flops 52609024 | bytes 8881184 | tf_op jit(solution)/shard_map/dot_general | solution.py:102
  354.4 7.2 %gather_fusion.12 = bf16[1536,640]{1,0:T(8,128)(2,1)} fusion(bf16[769,640]{1,0:T(8,128)(2,1)} %concatenate.20, s32[2048]{0:T(1024)S(1)} %pad_clamp_fusion.3), kind=kCustom, calls=%fused_computation.12 | custom fusion | bytes 3938304 | tf_op jit(solution)/shard_map/gather | solution.py:110
  366.0 7.2 %gather_fusion.13 = bf16[1536,640]{1,0:T(8,128)(2,1)} fusion(bf16[769,640]{1,0:T(8,128)(2,1)} %concatenate.20, s32[2048]{0:T(1024)S(1)} %pad_clamp_fusion.1), kind=kCustom, calls=%fused_computation.13 | custom fusion | bytes 3938304 | tf_op jit(solution)/shard_map/gather | solution.py:111
  373.2 31.6 %all-to-all-done.6 = bf16[8,192,640]{2,1,0:T(8,128)(2,1)} async-done(((bf16[8,192,640]{2,1,0:T(8,128)(2,1)}), bf16[8,192,640]{2,1,0:T(8,128)(2,1)}, u32[]{:S(2)}, u32[]{:S(2)}) %all-to-all-start.6) | async-done | bytes 1966112 | tf_op jit(solution)/shard_map/all_to_all | solution.py:113
  412.5 39.0 %all-to-all-done.7 = bf16[8,192,640]{2,1,0:T(8,128)(2,1)} async-done(((bf16[8,192,640]{2,1,0:T(8,128)(2,1)}), bf16[8,192,640]{2,1,0:T(8,128)(2,1)}, u32[]{:S(2)}, u32[]{:S(2)}) %all-to-all-start.7) | async-done | bytes 1966112 | tf_op jit(solution)/shard_map/all_to_all | solution.py:117
  457.4 10.7 %psum.41 = f32[4,640]{1,0:T(4,128)} all-reduce(f32[4,640]{1,0:T(4,128)S(1)} %reduce_sum.77), channel_id=1, replica_groups=mesh['shot'=8,'off'=4] {'off'}, use_global_device_ids=true, to_apply=%region_20.21 | all-reduce | flops 2560 | bytes 20480 | tf_op jit(solution)/shard_map/psum | solution.py:133
  470.3 35.6 %psum.42 = f32[8,640]{1,0:T(8,128)S(1)} all-reduce(f32[8,640]{1,0:T(8,128)S(1)} %fusion.30), channel_id=1, replica_groups=mesh['shot'=8,'off'=4] {'shot'}, use_global_device_ids=true, to_apply=%region_21.22 | all-reduce | flops 5120 | bytes 40960 | tf_op jit(solution)/shard_map/psum | solution.py:126
  (135 shorter events, 121.1 us)
Async XLA Ops:
  7.2 68.0 %copy-start = (bf16[4,192,2048]{2,1,0:T(8,128)(2,1)S(1)}, bf16[4,192,2048]{2,1,0:T(8,128)(2,1)}, u32[]{:S(2)}) copy-start(bf16[4,192,2048]{2,1,0:T(8,128)(2,1)} %param.8) | copy-start | bytes 9437188
  9.0 4.5 copy-start.2
  13.5 10.2 %copy-start.3 = (s32[4096]{0:T(1024)S(1)}, s32[4096]{0:T(1024)}, u32[]{:S(2)}) copy-start(s32[4096]{0:T(1024)} %param.15) | copy-start | bytes 49156
  34.0 8.1 %copy-start.4 = (s32[4096]{0:T(1024)S(1)}, s32[4096]{0:T(1024)}, u32[]{:S(2)}) copy-start(s32[4096]{0:T(1024)} %param.14) | copy-start | bytes 49156
  34.7 53.2 %all-to-all-start = ((s32[8,1,192]{2,1,0:T(1,128)}), s32[8,1,192]{2,1,0:T(1,128)S(1)}, u32[]{:S(2)}, u32[]{:S(2)}) async-start(s32[8,1,192]{2,1,0:T(1,128)} %all_to_all.32), calls=%async_computation | async-start | bytes 16384 | tf_op jit(solution)/shard_map/all_to_all | solution.py:114
  42.2 10.8 %copy-start.8 = (s32[4,192]{1,0:T(4,128)S(1)}, s32[4,192]{1,0:T(4,128)}, u32[]{:S(2)}) copy-start(s32[4,192]{1,0:T(4,128)} %param.9) | copy-start | bytes 9220
  87.9 18.8 %all-to-all-start.3 = ((s32[8,1,192]{2,1,0:T(1,128)}), s32[8,1,192]{2,1,0:T(1,128)S(1)}, u32[]{:S(2)}, u32[]{:S(2)}) async-start(s32[8,1,192]{2,1,0:T(1,128)} %all_to_all.36), calls=%async_computation.4 | async-start | bytes 16384 | tf_op jit(solution)/shard_map/all_to_all | solution.py:118
  106.7 50.4 %all-to-all-start.1 = ((bf16[8,192,640]{2,1,0:T(8,128)(2,1)}), bf16[8,192,640]{2,1,0:T(8,128)(2,1)}, u32[]{:S(2)}, u32[]{:S(2)}) async-start(bf16[8,192,640]{2,1,0:T(8,128)(2,1)} %bitcast.68), calls=%async_computation.1 | async-start | bytes 3932160 | tf_op jit(solution)/shard_map/all_to_all | solution.py:113
  157.1 49.4 %all-to-all-start.4 = ((bf16[8,192,640]{2,1,0:T(8,128)(2,1)}), bf16[8,192,640]{2,1,0:T(8,128)(2,1)}, u32[]{:S(2)}, u32[]{:S(2)}) async-start(bf16[8,192,640]{2,1,0:T(8,128)(2,1)} %bitcast.66), calls=%async_computation.5 | async-start | bytes 3932160 | tf_op jit(solution)/shard_map/all_to_all | solution.py:117
  161.4 27.2 %reduce-scatter.5.cloned.1.call-start = ((), (), s32[]{:S(2)}) async-start(), calls=%async_computation.12 | async-start | bytes 819200 | tf_op jit(solution)/shard_map/reduce_scatter | solution.py:135
  161.6 3.2 copy-start.13
  180.1 21.1 %copy-start.11 = (f32[64]{0:T(128)}, f32[64]{0:T(128)S(1)}, u32[]{:S(2)}) copy-start(f32[64]{0:T(128)S(1)} %dynamic-slice_add_fusion.1) | copy-start | bytes 772
  206.5 55.5 %all-to-all-start.2 = ((bf16[8,192,640]{2,1,0:T(8,128)(2,1)}), bf16[8,192,640]{2,1,0:T(8,128)(2,1)}, u32[]{:S(2)}, u32[]{:S(2)}) async-start(bf16[8,192,640]{2,1,0:T(8,128)(2,1)} %broadcast_select_fusion.1), calls=%async_computation.3 | async-start | bytes 3932160 | tf_op jit(solution)/shard_map/all_to_all | solution.py:152
  210.8 32.1 %reduce-scatter.7.cloned.1.call-start = ((), (), s32[]{:S(2)}) async-start(), calls=%async_computation.13 | async-start | bytes 1638400 | tf_op jit(solution)/shard_map/reduce_scatter | solution.py:137
  216.5 42.3 %copy-start.9 = (f32[128]{0:T(128)}, f32[128]{0:T(128)S(1)}, u32[]{:S(2)}) copy-start(f32[128]{0:T(128)S(1)} %dynamic-slice_add_fusion) | copy-start | bytes 1540
  262.0 80.2 %all-to-all-start.5 = ((bf16[8,192,640]{2,1,0:T(8,128)(2,1)}), bf16[8,192,640]{2,1,0:T(8,128)(2,1)}, u32[]{:S(2)}, u32[]{:S(2)}) async-start(bf16[8,192,640]{2,1,0:T(8,128)(2,1)} %broadcast_select_fusion), calls=%async_computation.7 | async-start | bytes 3932160 | tf_op jit(solution)/shard_map/all_to_all | solution.py:153
  267.5 69.2 %copy-start.7 = (s32[768]{0:T(1024)S(1)}, s32[768]{0:T(1024)}, u32[]{:S(2)}) copy-start(s32[768]{0:T(1024)} %copy-done.6) | copy-start | bytes 9220
  336.8 10.8 %copy-start.12 = (f32[8]{0:T(128)}, f32[8]{0:T(128)S(1)}, u32[]{:S(2)}) copy-start(f32[8]{0:T(128)S(1)} %broadcast_add_fusion) | copy-start | bytes 100
  361.6 43.2 %all-to-all-start.6 = ((bf16[8,192,640]{2,1,0:T(8,128)(2,1)}), bf16[8,192,640]{2,1,0:T(8,128)(2,1)}, u32[]{:S(2)}, u32[]{:S(2)}) async-start(bf16[8,192,640]{2,1,0:T(8,128)(2,1)} %bitcast.69), calls=%async_computation.8 | async-start | bytes 3932160 | tf_op jit(solution)/shard_map/all_to_all | solution.py:113
  404.8 46.7 %all-to-all-start.7 = ((bf16[8,192,640]{2,1,0:T(8,128)(2,1)}), bf16[8,192,640]{2,1,0:T(8,128)(2,1)}, u32[]{:S(2)}, u32[]{:S(2)}) async-start(bf16[8,192,640]{2,1,0:T(8,128)(2,1)} %bitcast.67), calls=%async_computation.10 | async-start | bytes 3932160 | tf_op jit(solution)/shard_map/all_to_all | solution.py:117
  409.2 99.5 %reduce-scatter.9.cloned.1.call-start = ((), (), s32[]{:S(2)}) async-start(), calls=%async_computation.14 | async-start | bytes 819200 | tf_op jit(solution)/shard_map/reduce_scatter | solution.py:135
  412.5 97.9 %reduce-scatter.11.cloned.1.call-start = ((), (), s32[]{:S(2)}) async-start(), calls=%async_computation.15 | async-start | bytes 1638400 | tf_op jit(solution)/shard_map/reduce_scatter | solution.py:137
  455.6 54.8 %copy-start.5 = (f32[128,640]{1,0:T(8,128)S(1)}, f32[128,640]{1,0:T(8,128)}, u32[]{:S(2)}) copy-start(f32[128,640]{1,0:T(8,128)} %reduce-scatter.7.cloned.1.call-done) | copy-start | bytes 983044
  455.6 54.7 %copy-start.10 = (f32[128]{0:T(128)S(1)}, f32[128]{0:T(128)}, u32[]{:S(2)}) copy-start(f32[128]{0:T(128)} %copy-done.9) | copy-start | bytes 1540
  (2 other events, 2.4 us)
Sparse Core Ops, SparseCore 0:
  164.9 23.6 reduce-scatter.4
  215.1 27.7 reduce-scatter.6
  412.6 23.3 reduce-scatter.8
  455.8 24.8 reduce-scatter.10
where the time goes:
time: 520 us; the launch traced here: 519 us
  waiting for transfers between devices  145 us (28%)
  blocking collectives  138 us (27%)
  local copies, waits for them, and re-layouts  96.2 us (18%)
  other arithmetic  46.1 us (9%)
  starting transfers between devices  42.3 us (8%)
  matrix products  35.5 us (7%)
  between operations  15.6 us (3%)
    psum x2, blocking collectives, shards(): bin_total, bin_number = lax.psum((bin_sums, bin_count), 'shot')  102 us
    all_to_all x2, waiting for transfers between devices, shards(): lax.all_to_all(rec_rows, 'shot', split_axis=0, concat_axis=0, tiled=True)  68.8 us
    all_to_all x2, waiting for transfers between devices, shards(): lax.all_to_all(cmp_rows, 'shot', split_axis=0, concat_axis=0, tiled=True)  41 us
    reduce_scatter x2, waiting for transfers between devices, shards(): lax.psum_scatter(cmp_sums, 'off', scatter_dimension=0, tiled=True)  26.4 us
    another operation x5, other arithmetic  25.9 us
    dot_general x4, matrix products, owner_totals(): jnp.dot(member.astype(jnp.bfloat16), rows, preferred_element_type=jnp.flo...  14.7 us
    gather x2, local copies, waits for them, and re-layouts, shards(): rec_rows = rounded[rec_source].reshape(n_shot, capacity, NF)  14.5 us
    gather x2, local copies, waits for them, and re-layouts, shards(): cmp_rows = rounded[cmp_source].reshape(n_shot, capacity, NF)  14.5 us
  transfers between devices with their start and end apart: 12, of which 6 were waited for; matrix products, arithmetic and copies ran while one was open for 25% of the time, Pallas kernels for 0%

commit v1 on v0

v1 whole, which is shorter than its diff:
```python
import math

import jax
import jax.numpy as jnp
from jax import lax
from jax.experimental import pallas as pl
from jax.experimental.pallas import tpu as pltpu
from jax.sharding import PartitionSpec as P

NF = 640
OFFB_DEV = 8
SWEEPS = 2
LANES = 128
WIDE = 256

OMEGA = 0.35
FLOOR = 0.05
VMEM_BYTES = 60 * 1024 * 1024


def up(value, unit):
    return -(-value // unit) * unit


def dot_nt(a, b):
    return lax.dot_general(a, b, (((1,), (1,)), ((), ())), preferred_element_type=jnp.float32)


def dot_nn(a, b):
    return lax.dot_general(a, b, (((1,), (0,)), ((), ())), preferred_element_type=jnp.float32)


def base_angles(samples, n_dev, held, padded):
    row = jnp.arange(n_dev * padded, dtype=jnp.int32)
    freq = ((row // padded) * held + row % padded)[:, None]
    coarse = jnp.arange(samples // LANES, dtype=jnp.int32)[None, :] * LANES
    fine = jnp.arange(LANES, dtype=jnp.int32)[None, :]
    step = 2.0 * math.pi / samples
    coarse_angle = (freq * coarse % samples).astype(jnp.float32) * step
    fine_angle = (freq * fine % samples).astype(jnp.float32) * step
    sample_idx = jnp.arange(samples, dtype=jnp.float32)[None, :]
    tapers = 0.5 - 0.5 * jnp.cos((sample_idx + 0.5) * step)
    weights = tapers * math.sqrt(8.0 / (3.0 * samples))
    return (
        jnp.cos(coarse_angle),
        jnp.sin(coarse_angle),
        jnp.cos(fine_angle),
        jnp.sin(fine_angle),
        weights,
    )


def logs_kernel(traces_ref, ca_ref, sa_ref, cb_ref, sb_ref, w_ref, out_ref, table):
    rows = ca_ref.shape[0]
    cb = cb_ref[...]
    sb = sb_ref[...]
    for a in range(traces_ref.shape[1] // LANES):
        cols = slice(a * LANES, (a + 1) * LANES)
        w = w_ref[:, cols]
        ca = ca_ref[:, a : a + 1]
        sa = sa_ref[:, a : a + 1]
        table[:rows, cols] = (w * (ca * cb - sa * sb)).astype(jnp.bfloat16)
        table[rows:, cols] = (-w * (sa * cb + ca * sb)).astype(jnp.bfloat16)
    products = dot_nt(table[...], traces_ref[...])
    real_part = products[:rows]
    imag_part = products[rows:]
    logs = jnp.log(real_part * real_part + imag_part * imag_part + FLOOR)
    out_ref[...] = logs.astype(jnp.bfloat16).reshape(out_ref.shape)


def log_blocks(traces, n_dev, held, padded):
    tr_dev, samples = traces.shape
    groups = 4 if n_dev % 4 == 0 else 1
    dests = n_dev // groups
    rows = dests * padded
    ca, sa, cb, sb, w = base_angles(samples, n_dev, held, padded)
    part = lambda width: pl.BlockSpec((rows, width), lambda g: (g, 0))
    whole = lambda shape: pl.BlockSpec(shape, lambda g: (0, 0))
    return pl.pallas_call(
        logs_kernel,
        grid=(groups,),
        out_shape=jax.ShapeDtypeStruct((n_dev, padded, tr_dev), jnp.bfloat16),
        in_specs=[
            whole((tr_dev, samples)),
            part(ca.shape[1]),
            part(ca.shape[1]),
            part(LANES),
            part(LANES),
            whole((1, samples)),
        ],
        out_specs=pl.BlockSpec((dests, padded, tr_dev), lambda g: (g, 0, 0)),
        scratch_shapes=[pltpu.VMEM((2 * rows, samples), jnp.bfloat16)],
        compiler_params=pltpu.CompilerParams(vmem_limit_bytes=VMEM_BYTES),
        name="logs",
    )(traces, ca, sa, cb, sb, w)


def one_hot(index, count):
    rows = lax.broadcasted_iota(jnp.int32, (count, index.shape[1]), 0)
    return jnp.where(rows == index, 1.0, 0.0).astype(jnp.bfloat16)


def level_mask(index, levels, rows):
    level = lax.broadcasted_iota(jnp.int32, (levels, rows, index.shape[1]), 0)
    return level == index[None]


def spread(values, mask):
    levels, rows, width = mask.shape
    return jnp.where(mask, values[None], 0.0).astype(jnp.bfloat16).reshape(levels * rows, width)


def split_float(values):
    high = values.astype(jnp.bfloat16)
    low = (values - high.astype(jnp.float32)).astype(jnp.bfloat16)
    return jnp.concatenate([high, low], axis=0)


def sweeps_kernel(
    sizes,
    logs_ref,
    ids_ref,
    rec_owner_ref,
    rec_slot_ref,
    cmp_owner_ref,
    cmp_slot_ref,
    out_ref,
    rec_acc,
    cmp_acc,
    so_acc,
    rec_x,
    cmp_x,
    so_x,
    rec_b,
    cmp_b,
    placed,
):
    n_shot, n_off, shot_dev, held, rec_dev, cmp_dev = sizes
    n_dev, padded, tr_dev = logs_ref.shape
    tr_off = tr_dev // shot_dev
    n_bins = n_off * OFFB_DEV
    rec_l = rec_acc.shape[0] // padded
    cmp_l = cmp_acc.shape[0] // padded
    so_width = so_acc.shape[1]
    freq_row = lax.broadcasted_iota(jnp.int32, (padded, tr_dev), 0)
    local_shot = lax.broadcasted_iota(jnp.int32, (1, tr_dev), 1) // tr_off

    def sums_over_traces(first):
        rec_acc[...] = jnp.zeros_like(rec_acc)
        cmp_acc[...] = jnp.zeros_like(cmp_acc)
        so_acc[...] = jnp.zeros_like(so_acc)

        @pl.loop(0, n_dev)
        def _(src):
            ids = ids_ref[src]
            rec = ids[1:2]
            cmp = ids[2:3]
            shot = (src // n_off) * shot_dev + local_shot + n_bins
            so_row = lax.broadcasted_iota(jnp.int32, (so_width, tr_dev), 0)
            so_hot = jnp.where((so_row == ids[0:1]) | (so_row == shot), 1.0, 0.0).astype(
                jnp.bfloat16
            )
            rec_hot = one_hot(rec % WIDE, WIDE)
            cmp_hot = one_hot(cmp % WIDE, WIDE)
            rec_mask = level_mask(rec // WIDE, rec_l, padded)
            cmp_mask = level_mask(cmp // WIDE, cmp_l, padded)
            values = logs_ref[src].astype(jnp.float32)
            if first:
                values = jnp.where(freq_row == held, 1.0, values)
            else:
                so_part = dot_nn(so_x[...], so_hot)
                rec_part = dot_nn(rec_x[...], rec_hot).reshape(rec_mask.shape)
                cmp_part = dot_nn(cmp_x[...], cmp_hot).reshape(cmp_mask.shape)
                values = values - (so_part[:padded] + so_part[padded:])
                values = values - jnp.sum(jnp.where(rec_mask, rec_part, 0.0), axis=0)
                values = values - jnp.sum(jnp.where(cmp_mask, cmp_part, 0.0), axis=0)
            rec_acc[...] += dot_nt(spread(values, rec_mask), rec_hot)
            cmp_acc[...] += dot_nt(spread(values, cmp_mask), cmp_hot)
            so_sums = dot_nt(split_float(values), so_hot)
            so_acc[...] += so_sums[:padded] + so_sums[padded:]

    def update(sums, counts, levels):
        shaped = sums.reshape(levels, padded, sums.shape[1])
        number = counts.reshape(shaped.shape)[:, held : held + 1, :]
        return OMEGA * shaped / (number + 1.0)

    sums_over_traces(True)
    rec_counts, cmp_counts, so_counts = rec_b, cmp_b, placed
    rec_counts[...] = rec_acc[...]
    cmp_counts[...] = cmp_acc[...]
    so_first = update(so_acc[...], so_acc[...], 1).reshape(padded, so_width)
    so_number = so_acc[held : held + 1, :]
    rec_x[...] = update(rec_acc[...], rec_acc[...], rec_l).reshape(rec_x.shape).astype(jnp.bfloat16)
    cmp_x[...] = update(cmp_acc[...], cmp_acc[...], cmp_l).reshape(cmp_x.shape).astype(jnp.bfloat16)
    so_x[...] = split_float(so_first)
    for _ in range(SWEEPS - 1):
        sums_over_traces(False)
    rec_acc[...] = update(rec_acc[...] + rec_counts[...], rec_counts[...], rec_l).reshape(
        rec_acc.shape
    )
    cmp_acc[...] = update(cmp_acc[...] + cmp_counts[...], cmp_counts[...], cmp_l).reshape(
        cmp_acc.shape
    )
    so_final = so_first + OMEGA * so_acc[...] / (so_number + 1.0)

    rec_rows = rec_dev // n_off
    cmp_rows = cmp_dev // n_off
    columns = out_ref.shape[2]
    placed[...] = jnp.zeros_like(placed)

    def place(values, dest, column):
        mask = level_mask(dest, n_dev, padded)
        placed[...] += dot_nt(spread(values, mask), one_hot(column, columns))

    @pl.loop(0, rec_l)
    def _(level):
        position = rec_owner_ref[pl.ds(level, 1)] * rec_dev + rec_slot_ref[pl.ds(level, 1)]
        values = rec_acc[pl.ds(pl.multiple_of(level * padded, 8), padded), :]
        place(values, position // rec_rows, position % rec_rows)

    @pl.loop(0, cmp_l)
    def _(level):
        position = cmp_owner_ref[pl.ds(level, 1)] * cmp_dev + cmp_slot_ref[pl.ds(level, 1)]
        values = cmp_acc[pl.ds(pl.multiple_of(level * padded, 8), padded), :]
        place(values, position // cmp_rows, position % cmp_rows + rec_rows)

    item = lax.broadcasted_iota(jnp.int32, (1, so_width), 1)
    shot = item - n_bins
    is_bin = item < n_bins
    base = rec_rows + cmp_rows
    column = jnp.where(is_bin, base + item % OFFB_DEV, base + OFFB_DEV + shot % shot_dev)
    dest = lax.broadcasted_iota(jnp.int32, (n_dev, padded, so_width), 0)
    items = lax.broadcasted_iota(jnp.int32, (n_dev, padded, so_width), 2)
    mask = jnp.where(items < n_bins, dest % n_off, dest // n_off) == jnp.where(
        items < n_bins, items // OFFB_DEV, (items - n_bins) // shot_dev
    )
    placed[...] += dot_nt(spread(so_final, mask), one_hot(column, columns))
    out_ref[...] = placed[...].astype(jnp.bfloat16).reshape(out_ref.shape)


def run_sweeps(logs, ids, rec_owner, rec_slot, cmp_owner, cmp_slot, sizes, columns):
    n_shot, n_off, shot_dev, _, _, _ = sizes
    n_dev, padded, _ = logs.shape
    rec_l = rec_owner.shape[0]
    cmp_l = cmp_owner.shape[0]
    so_width = up(n_shot * shot_dev + n_off * OFFB_DEV, LANES)
    return pl.pallas_call(
        lambda *refs: sweeps_kernel(sizes, *refs),
        out_shape=jax.ShapeDtypeStruct((n_dev, padded, columns), jnp.bfloat16),
        in_specs=[pl.BlockSpec(memory_space=pltpu.VMEM)] * 6,
        out_specs=pl.BlockSpec(memory_space=pltpu.VMEM),
        scratch_shapes=[
            pltpu.VMEM((rec_l * padded, WIDE), jnp.float32),
            pltpu.VMEM((cmp_l * padded, WIDE), jnp.float32),
            pltpu.VMEM((padded, so_width), jnp.float32),
            pltpu.VMEM((rec_l * padded, WIDE), jnp.bfloat16),
            pltpu.VMEM((cmp_l * padded, WIDE), jnp.bfloat16),
            pltpu.VMEM((2 * padded, so_width), jnp.bfloat16),
            pltpu.VMEM((rec_l * padded, WIDE), jnp.float32),
            pltpu.VMEM((cmp_l * padded, WIDE), jnp.float32),
            pltpu.VMEM((n_dev * padded, columns), jnp.float32),
        ],
        compiler_params=pltpu.CompilerParams(vmem_limit_bytes=VMEM_BYTES),
        name="sweeps",
    )(logs, ids, rec_owner, rec_slot, cmp_owner, cmp_slot)


def shards(traces, offset_bin, rec_id, cmp_id, rec_owner, rec_slot, cmp_owner, cmp_slot):
    shot_dev, tr_off, samples = traces.shape
    n_shot = lax.axis_size("shot")
    n_off = lax.axis_size("off")
    n_dev = n_shot * n_off
    axes = ("shot", "off")
    tr_dev = shot_dev * tr_off
    rec_dev = rec_owner.shape[0] // n_shot
    cmp_dev = cmp_owner.shape[0] // n_shot
    rec_rows = rec_dev // n_off
    cmp_rows = cmp_dev // n_off
    held = up(NF, n_dev) // n_dev
    padded = up(held + 1, 8)
    columns = up(rec_rows + cmp_rows + shot_dev + OFFB_DEV, LANES)
    local_ids = jnp.stack(
        [offset_bin.reshape(tr_dev), rec_id.reshape(tr_dev), cmp_id.reshape(tr_dev)]
    )
    ids = lax.all_gather(local_ids, axes, axis=0)
    blocks = log_blocks(traces.reshape(tr_dev, samples), n_dev, held, padded)
    logs = lax.all_to_all(blocks, axes, split_axis=0, concat_axis=0, tiled=True)
    sizes = (n_shot, n_off, shot_dev, held, rec_dev, cmp_dev)
    wide = lambda table: table.reshape(-1, WIDE)
    terms = run_sweeps(
        logs, ids, wide(rec_owner), wide(rec_slot), wide(cmp_owner), wide(cmp_slot), sizes, columns
    )
    parts = lax.all_to_all(terms, axes, split_axis=0, concat_axis=0, tiled=True)
    held_rows = parts[:, :held].reshape(n_dev * held, columns)[:NF]
    rows = held_rows.astype(jnp.float32).T
    base = rec_rows + cmp_rows
    return (
        rows[base + OFFB_DEV : base + OFFB_DEV + shot_dev],
        rows[base : base + OFFB_DEV],
        rows[:rec_rows],
        rows[rec_rows:base],
    )


def solution(mesh):
    return jax.shard_map(
        shards,
        mesh=mesh,
        in_specs=(
            P("shot", "off", None),
            P("shot", "off"),
            P("shot", "off"),
            P("shot", "off"),
            P(),
            P(),
            P(),
            P(),
        ),
        out_specs=(
            P("shot", None),
            P("off", None),
            P(("shot", "off"), None),
            P(("shot", "off"), None),
        ),
        check_vma=False,
    )
```

time: 520 us -> 164 us (0.32)
  waiting for transfers between devices: 145 us -> 0.01 us
  local copies, waits for them, and re-layouts: 96.2 us -> 7.61 us
  Pallas kernels: 0 us -> 70.4 us
  blocking collectives: 138 us -> 71.4 us
  other arithmetic: 46.1 us -> 5.8 us
  matrix products: 35.5 us -> 0 us
  starting transfers between devices: 42.3 us -> 7.33 us
  between operations: 15.6 us -> 0.77 us
    psum x3 -> x0, blocking collectives: 113 us -> none  [the longest x2 102 us: shards(): bin_total, bin_number = lax.psum((bin_sums, bin_count), 'shot')]
    all_to_all x8 -> x1, waiting for transfers between devices: 110 us -> 0.01 us  [shards(): logs = lax.all_to_all(blocks, axes, split_axis=0, concat_axis=0, tiled=True)]
    gather x14 -> x0, local copies, waits for them, and re-layouts: 81.9 us -> none  [the longest x2 14.5 us: shards(): rec_rows = rounded[rec_source].reshape(n_shot, capacity, NF)]
    pallas_call x0 -> x2, Pallas kernels: none -> 70.4 us  [the longest x1 58.1 us: run_sweeps(): pl.pallas_call(lambda *refs: sweeps_kernel(sizes, *refs), out_shape=jax.S...]
    all_gather x2 -> x1, blocking collectives: 13.7 us -> 55.6 us  [shards(): ids = lax.all_gather(local_ids, axes, axis=0)]
    dot_general x9 -> x0, matrix products: 35.5 us -> none  [the longest x4 14.7 us: owner_totals(): jnp.dot(member.astype(jnp.bfloat16), rows, preferred_element_type=jnp.flo...]
    reduce_scatter x4 -> x0, waiting for transfers between devices: 34.9 us -> none  [the longest x2 26.4 us: shards(): lax.psum_scatter(cmp_sums, 'off', scatter_dimension=0, tiled=True)]
    all_to_all x8 -> x1, starting transfers between devices: 42.1 us -> 7.33 us  [shards(): logs = lax.all_to_all(blocks, axes, split_axis=0, concat_axis=0, tiled=True)]
  transfers between devices with their start and end apart: 12 -> 1, of which waited for: 6 -> 0; matrix products, arithmetic and copies ran while one was open for 25% -> 2% of each run, Pallas kernels for 0% -> 0%
where the time goes in v1:
time: 164 us; the launch traced here: 163 us
  blocking collectives  71.4 us (44%)
  Pallas kernels  70.4 us (43%)
  local copies, waits for them, and re-layouts  7.61 us (5%)
  starting transfers between devices  7.33 us (4%)
  other arithmetic  5.8 us (4%)
    pallas_call x1, Pallas kernels, run_sweeps(): pl.pallas_call(lambda *refs: sweeps_kernel(sizes, *refs), out_shape=jax.S...  58.1 us
    all_gather x1, blocking collectives, shards(): ids = lax.all_gather(local_ids, axes, axis=0)  55.6 us
    all_to_all x1, blocking collectives, shards(): parts = lax.all_to_all(terms, axes, split_axis=0, concat_axis=0, tiled=True)  15.8 us
    pallas_call x1, Pallas kernels, log_blocks(): pl.pallas_call(logs_kernel, grid=(groups,), out_shape=jax.ShapeDtypeStruc...  12.3 us
    all_to_all x1, starting transfers between devices, shards(): logs = lax.all_to_all(blocks, axes, split_axis=0, concat_axis=0, tiled=True)  7.33 us
    unnamed x20, local copies, waits for them, and re-layouts  4.25 us
  transfers between devices with their start and end apart: 1, of which 0 were waited for; matrix products, arithmetic and copies ran while one was open for 2% of the time, Pallas kernels for 0%

profile of v1, /device:TPU:0, one launch (start us, length us, event | category | flops | bytes accessed | tf_op | source)
XLA Modules:
  0.0 163.3 jit_solution(9917546670930908010)
XLA Ops:
  0.7 0.9 subtract_multiply_fusion.w_ref
  1.5 2.6 %fusion.6 = (f32[768,128]{1,0:T(8,128)}, f32[768,128]{1,0:T(8,128)}) fusion(s32[768]{0:T(1024)S(1)} %fusion.17), kind=kLoop, calls=%fused_computation.12 | loop fusion | flops 1376256 | bytes 789504 | tf_op jit(solution)/shard_map/sin | solution.py:48
  4.1 0.1 fusion.8
  4.2 0.2 copy.21
  4.4 2.2 %multiply_sine_fusion = (f32[768,16]{1,0:T(8,128)}, f32[768,16]{1,0:T(8,128)}) fusion(f32[768,16]{1,0:T(8,128)S(1)} %copy.21), kind=kLoop, calls=%fused_computation.10 | loop fusion | flops 12288 | bytes 147456 | tf_op jit(solution)/shard_map/sin | solution.py:46
  6.5 12.3 %logs.1 = bf16[32,24,768]{2,1,0:T(8,128)(2,1)} custom-call(bf16[768,2048]{1,0:T(8,128)(2,1)} %bitcast.8, f32[768,16]{1,0:T(8,128)} %get-tuple-element.17.ca_ref, f32[768,16]{1,0:T(8,128)} %get-tuple-element.16.sa_ref, f32[768,128]{1,0:T(8,128)} %get-tuple-element.19.cb_ref, f32[768,128]{1,0:T(8,128)} %get-tuple-element.18.sb_ref, ...), custom_call_target="tpu_custom_call" | custom-call | tf_op jit(solution)/shard_map/logs/pallas_call | solution.py:79
  18.9 7.3 %all-to-all-start = ((bf16[32,24,768]{2,1,0:T(8,128)(2,1)}), bf16[32,24,768]{2,1,0:T(8,128)(2,1)S(1)}, u32[]{:S(2)}, u32[]{:S(2)}) async-start(bf16[32,24,768]{2,1,0:T(8,128)(2,1)} %logs.1), calls=%async_computation | async-start | bytes 2359296 | tf_op jit(solution)/shard_map/all_to_all | solution.py:287
  26.3 0.1 stack_reshape.10
  26.4 0.1 stack_reshape.11
  26.5 0.6 reshape.81.refs_4_
  27.2 0.6 reshape.82.refs_5_
  27.8 0.6 reshape.79.refs_2_
  28.4 0.6 reshape.80.refs_3_
  29.0 55.6 %all-gather.1.refs_1_ = s32[32,3,768]{2,1,0:T(4,128)} all-gather(s32[1,3,768]{2,1,0:T(4,128)S(1)} %add_bitcast_fusion), channel_id=2, replica_groups=mesh['shot'=8,'off'=4] {'shot','off'}, dimensions={0}, use_global_device_ids=true | all-gather | bytes 304128 | tf_op jit(solution)/shard_map/all_gather | solution.py:285
  84.6 1.0 copy-done
  85.6 58.1 %sweeps.1 = bf16[32,24,256]{2,1,0:T(8,128)(2,1)} custom-call(bf16[32,24,768]{2,1,0:T(8,128)(2,1)} %copy-done, s32[32,3,768]{2,1,0:T(4,128)} %all-gather.1.refs_1_, s32[8,256]{1,0:T(8,128)} %reshape.79.refs_2_, s32[8,256]{1,0:T(8,128)} %reshape.80.refs_3_, s32[16,256]{1,0:T(8,128)} %reshape.81.refs_4_, s32[16,256]{1,0:T(8,128)} %reshape.82.refs_5_), custom_call_target="tpu_custom_call" | custom-call | tf_op jit(solution)/shard_map/sweeps/pallas_call | solution.py:247
  143.7 15.8 %all_to_all.10 = bf16[32,24,256]{2,1,0:T(8,128)(2,1)S(1)} all-to-all(bf16[32,24,256]{2,1,0:T(8,128)(2,1)} %sweeps.1), channel_id=1, replica_groups=mesh['shot'=8,'off'=4] {'shot','off'}, dimensions={0} | all-to-all | bytes 786432 | tf_op jit(solution)/shard_map/all_to_all | solution.py:293
  159.7 0.1 slice.24
  159.8 0.1 slice.22
  160.0 0.1 slice.21
  160.1 0.9 copy.25
  161.0 0.8 copy.24
  161.9 0.7 copy.23
  162.6 0.7 copy.22
  (23 shorter events, 0.3 us)
Async XLA Ops:
  18.9 7.4 %copy-start.5 = (s32[4,192]{1,0:T(4,128)S(1)}, s32[4,192]{1,0:T(4,128)}, u32[]{:S(2)}) copy-start(s32[4,192]{1,0:T(4,128)} %param.10) | copy-start | bytes 9220
  18.9 7.5 %copy-start.6 = (s32[4,192]{1,0:T(4,128)S(1)}, s32[4,192]{1,0:T(4,128)}, u32[]{:S(2)}) copy-start(s32[4,192]{1,0:T(4,128)} %param.11) | copy-start | bytes 9220
  18.9 7.6 %copy-start.7 = (s32[4,192]{1,0:T(4,128)S(1)}, s32[4,192]{1,0:T(4,128)}, u32[]{:S(2)}) copy-start(s32[4,192]{1,0:T(4,128)} %param.9) | copy-start | bytes 9220
  18.9 7.7 %copy-start.1 = (s32[4096]{0:T(1024)S(1)}, s32[4096]{0:T(1024)}, u32[]{:S(2)}) copy-start(s32[4096]{0:T(1024)} %param.14) | copy-start | bytes 49156
  18.9 8.3 %copy-start.2 = (s32[4096]{0:T(1024)S(1)}, s32[4096]{0:T(1024)}, u32[]{:S(2)}) copy-start(s32[4096]{0:T(1024)} %param.15) | copy-start | bytes 49156
  18.9 8.9 %copy-start.3 = (s32[2048]{0:T(1024)S(1)}, s32[2048]{0:T(1024)}, u32[]{:S(2)}) copy-start(s32[2048]{0:T(1024)} %param.12) | copy-start | bytes 24580
  18.9 9.5 %copy-start.4 = (s32[2048]{0:T(1024)S(1)}, s32[2048]{0:T(1024)}, u32[]{:S(2)}) copy-start(s32[2048]{0:T(1024)} %param.13) | copy-start | bytes 24580
  18.9 65.7 %all-to-all-start = ((bf16[32,24,768]{2,1,0:T(8,128)(2,1)}), bf16[32,24,768]{2,1,0:T(8,128)(2,1)S(1)}, u32[]{:S(2)}, u32[]{:S(2)}) async-start(bf16[32,24,768]{2,1,0:T(8,128)(2,1)} %logs.1), calls=%async_computation | async-start | bytes 2359296 | tf_op jit(solution)/shard_map/all_to_all | solution.py:287
  84.6 1.0 copy-start

commit v2 on v1

--- a/solution.py
+++ b/solution.py
@@ -2,6 +2,7 @@
 
 import jax
 import jax.numpy as jnp
+import numpy as np
 from jax import lax
 from jax.experimental import pallas as pl
 from jax.experimental.pallas import tpu as pltpu
@@ -31,68 +32,244 @@
 
 
 def base_angles(samples, n_dev, held, padded):
-    row = jnp.arange(n_dev * padded, dtype=jnp.int32)
+    row = np.arange(n_dev * padded)
     freq = ((row // padded) * held + row % padded)[:, None]
-    coarse = jnp.arange(samples // LANES, dtype=jnp.int32)[None, :] * LANES
-    fine = jnp.arange(LANES, dtype=jnp.int32)[None, :]
     step = 2.0 * math.pi / samples
-    coarse_angle = (freq * coarse % samples).astype(jnp.float32) * step
-    fine_angle = (freq * fine % samples).astype(jnp.float32) * step
-    sample_idx = jnp.arange(samples, dtype=jnp.float32)[None, :]
-    tapers = 0.5 - 0.5 * jnp.cos((sample_idx + 0.5) * step)
+    coarse = freq * (np.arange(samples // LANES)[None, :] * LANES) % samples * step
+    fine = freq * np.arange(LANES)[None, :] % samples * step
+    tapers = 0.5 - 0.5 * np.cos((np.arange(samples)[None, :] + 0.5) * step)
     weights = tapers * math.sqrt(8.0 / (3.0 * samples))
-    return (
-        jnp.cos(coarse_angle),
-        jnp.sin(coarse_angle),
-        jnp.cos(fine_angle),
-        jnp.sin(fine_angle),
-        weights,
-    )
-
-
-def logs_kernel(traces_ref, ca_ref, sa_ref, cb_ref, sb_ref, w_ref, out_ref, table):
-    rows = ca_ref.shape[0]
-    cb = cb_ref[...]
-    sb = sb_ref[...]
-    for a in range(traces_ref.shape[1] // LANES):
-        cols = slice(a * LANES, (a + 1) * LANES)
-        w = w_ref[:, cols]
-        ca = ca_ref[:, a : a + 1]
-        sa = sa_ref[:, a : a + 1]
-        table[:rows, cols] = (w * (ca * cb - sa * sb)).astype(jnp.bfloat16)
-        table[rows:, cols] = (-w * (sa * cb + ca * sb)).astype(jnp.bfloat16)
-    products = dot_nt(table[...], traces_ref[...])
-    real_part = products[:rows]
-    imag_part = products[rows:]
-    logs = jnp.log(real_part * real_part + imag_part * imag_part + FLOOR)
-    out_ref[...] = logs.astype(jnp.bfloat16).reshape(out_ref.shape)
-
-
-def log_blocks(traces, n_dev, held, padded):
+    tables = (np.cos(coarse), np.sin(coarse), np.cos(fine), np.sin(fine), weights)
+    return tuple(table.astype(np.float32) for table in tables)
+
+
+def my_position(n_off):
+    return lax.axis_index("shot") * n_off + lax.axis_index("off")
+
+
+def remote(src, dst, send_sem, recv_sem, dest, n_off):
+    return pltpu.make_async_remote_copy(
+        src_ref=src,
+        dst_ref=dst,
+        send_sem=send_sem,
+        recv_sem=recv_sem,
+        device_id=(dest // n_off, dest % n_off),
+        device_id_type=pl.DeviceIdType.MESH,
+    )
+
+
+def greet_all(me, n_dev, n_off):
+    barrier = pltpu.get_barrier_semaphore()
+
+    @pl.loop(1, n_dev)
+    def _(step):
+        dest = (me + step) % n_dev
+        pl.semaphore_signal(
+            barrier,
+            inc=1,
+            device_id=(dest // n_off, dest % n_off),
+            device_id_type=pl.DeviceIdType.MESH,
+        )
+
+    return barrier
+
+
+def logs_kernel(
+    n_off,
+    groups,
+    traces_ref,
+    ids_ref,
+    ca_ref,
+    sa_ref,
+    cb_ref,
+    sb_ref,
+    w_ref,
+    out_ref,
+    ids_out_ref,
+    stage,
+    table,
+    send_sems,
+    recv_sems,
+    id_send_sems,
+    id_recv_sems,
+    own_sems,
+):
+    n_dev, padded, tr_dev = out_ref.shape
+    dests = n_dev // groups
+    rows = dests * padded
+    me = my_position(n_off)
+    barrier = greet_all(me, n_dev, n_off)
+
+    def block_copy(dest, slot):
+        return remote(
+            stage.at[dest], out_ref.at[slot], send_sems.at[dest], recv_sems.at[slot], dest, n_off
+        )
+
+    def id_copy(dest, slot):
+        return remote(
+            ids_ref, ids_out_ref.at[slot], id_send_sems.at[dest], id_recv_sems.at[slot], dest, n_off
+        )
+
+    own_ids = pltpu.make_async_copy(ids_ref, ids_out_ref.at[me], own_sems.at[0])
+    own_ids.start()
+    for turn in range(groups):
+        group = ((me // dests) + groups - 1 - turn) % groups
+        if groups & (groups - 1) == 0:
+            group = (me // dests) ^ (groups - 1 - turn)
+        base = pl.multiple_of(group * rows, 8)
+        cb = cb_ref[pl.ds(base, rows), :]
+        sb = sb_ref[pl.ds(base, rows), :]
+        ca_all = ca_ref[pl.ds(base, rows), :]
+        sa_all = sa_ref[pl.ds(base, rows), :]
+        for a in range(traces_ref.shape[1] // LANES):
+            cols = slice(a * LANES, (a + 1) * LANES)
+            w = w_ref[:, cols]
+            ca = ca_all[:, a : a + 1]
+            sa = sa_all[:, a : a + 1]
+            table[:rows, cols] = (w * (ca * cb - sa * sb)).astype(jnp.bfloat16)
+            table[rows:, cols] = (-w * (sa * cb + ca * sb)).astype(jnp.bfloat16)
+        products = dot_nt(table[...], traces_ref[...])
+        real_part = products[:rows]
+        imag_part = products[rows:]
+        logs = jnp.log(real_part * real_part + imag_part * imag_part + FLOOR)
+        stage[pl.ds(group * dests, dests)] = logs.astype(jnp.bfloat16).reshape(
+            dests, padded, tr_dev
+        )
+        if turn == 0:
+            pl.semaphore_wait(barrier, n_dev - 1)
+
+        @pl.loop(0, dests)
+        def _(step):
+            dest = group * dests + (step + me) % dests
+
+            @pl.when(dest != me)
+            def _():
+                block_copy(dest, me).start()
+
+        if turn == 0:
+
+            @pl.loop(1, n_dev)
+            def _(step):
+                id_copy((me + step) % n_dev, me).start()
+
+    own = pltpu.make_async_copy(stage.at[me], out_ref.at[me], own_sems.at[1])
+    own.start()
+
+    @pl.loop(1, n_dev)
+    def _(step):
+        dest = (me + step) % n_dev
+        block_copy(dest, me).wait_send()
+        id_copy(dest, me).wait_send()
+        block_copy(dest, dest).wait_recv()
+        id_copy(dest, dest).wait_recv()
+
+    own.wait()
+    own_ids.wait()
+
+
+def log_blocks(traces, ids, n_off, n_dev, held, padded):
     tr_dev, samples = traces.shape
     groups = 4 if n_dev % 4 == 0 else 1
-    dests = n_dev // groups
-    rows = dests * padded
-    ca, sa, cb, sb, w = base_angles(samples, n_dev, held, padded)
-    part = lambda width: pl.BlockSpec((rows, width), lambda g: (g, 0))
-    whole = lambda shape: pl.BlockSpec(shape, lambda g: (0, 0))
+    rows = n_dev // groups * padded
+    tables = base_angles(samples, n_dev, held, padded)
+    vmem = pl.BlockSpec(memory_space=pltpu.VMEM)
     return pl.pallas_call(
-        logs_kernel,
-        grid=(groups,),
-        out_shape=jax.ShapeDtypeStruct((n_dev, padded, tr_dev), jnp.bfloat16),
-        in_specs=[
-            whole((tr_dev, samples)),
-            part(ca.shape[1]),
-            part(ca.shape[1]),
-            part(LANES),
-            part(LANES),
-            whole((1, samples)),
+        lambda *refs: logs_kernel(n_off, groups, *refs),
+        out_shape=(
+            jax.ShapeDtypeStruct((n_dev, padded, tr_dev), jnp.bfloat16),
+            jax.ShapeDtypeStruct((n_dev,) + ids.shape, ids.dtype),
+        ),
+        in_specs=[vmem] * 7,
+        out_specs=(vmem, vmem),
+        scratch_shapes=[
+            pltpu.VMEM((n_dev, padded, tr_dev), jnp.bfloat16),
+            pltpu.VMEM((2 * rows, samples), jnp.bfloat16),
+            pltpu.SemaphoreType.DMA((n_dev,)),
+            pltpu.SemaphoreType.DMA((n_dev,)),
+            pltpu.SemaphoreType.DMA((n_dev,)),
+            pltpu.SemaphoreType.DMA((n_dev,)),
+            pltpu.SemaphoreType.DMA((2,)),
         ],
-        out_specs=pl.BlockSpec((dests, padded, tr_dev), lambda g: (g, 0, 0)),
-        scratch_shapes=[pltpu.VMEM((2 * rows, samples), jnp.bfloat16)],
-        compiler_params=pltpu.CompilerParams(vmem_limit_bytes=VMEM_BYTES),
+        compiler_params=pltpu.CompilerParams(
+            vmem_limit_bytes=VMEM_BYTES, collective_id=0, has_side_effects=True
+        ),
         name="logs",
-    )(traces, ca, sa, cb, sb, w)
+    )(traces, ids, *tables)
+
+
+def return_kernel(
+    n_off,
+    splits,
+    terms_ref,
+    source_ref,
+    offset_ref,
+    rec_ref,
+    cmp_ref,
+    landed,
+    joined,
+    send_sems,
+    recv_sems,
+    own_sem,
+):
+    n_dev = terms_ref.shape[0]
+    held = -(-source_ref.shape[1] // n_dev)
+    me = my_position(n_off)
+    barrier = greet_all(me, n_dev, n_off)
+
+    def block_copy(dest, slot):
+        return remote(
+            terms_ref.at[dest], landed.at[slot], send_sems.at[dest], recv_sems.at[slot], dest, n_off
+        )
+
+    own = pltpu.make_async_copy(terms_ref.at[me], landed.at[me], own_sem)
+    own.start()
+    pl.semaphore_wait(barrier, n_dev - 1)
+
+    @pl.loop(1, n_dev)
+    def _(step):
+        block_copy((me + step) % n_dev, me).start()
+
+    @pl.loop(1, n_dev)
+    def _(step):
+        dest = (me + step) % n_dev
+        block_copy(dest, me).wait_send()
+        block_copy(dest, dest).wait_recv()
+
+    own.wait()
+    for src in range(n_dev):
+        rows = min(held, joined.shape[0] - src * held)
+        if rows > 0:
+            joined[src * held : src * held + rows, :] = landed[src].astype(jnp.float32)[:rows]
+    turned = joined[...].T
+    a, b, c, d = splits
+    rec_ref[...] = turned[:a]
+    cmp_ref[...] = turned[a:b]
+    offset_ref[...] = turned[b:c]
+    source_ref[...] = turned[c:d]
+
+
+def return_terms(terms, n_off, splits):
+    n_dev, padded, columns = terms.shape
+    a, b, c, d = splits
+    vmem = pl.BlockSpec(memory_space=pltpu.VMEM)
+    shape = lambda rows: jax.ShapeDtypeStruct((rows, NF), jnp.float32)
+    return pl.pallas_call(
+        lambda *refs: return_kernel(n_off, splits, *refs),
+        out_shape=(shape(d - c), shape(c - b), shape(a), shape(b - a)),
+        in_specs=[vmem],
+        out_specs=(vmem,) * 4,
+        scratch_shapes=[
+            pltpu.VMEM((n_dev, padded, columns), jnp.bfloat16),
+            pltpu.VMEM((NF, columns), jnp.float32),
+            pltpu.SemaphoreType.DMA((n_dev,)),
+            pltpu.SemaphoreType.DMA((n_dev,)),
+            pltpu.SemaphoreType.DMA,
+        ],
+        compiler_params=pltpu.CompilerParams(
+            vmem_limit_bytes=VMEM_BYTES, collective_id=1, has_side_effects=True
+        ),
+        name="returns",
+    )(terms)
 
 
 def one_hot(index, count):
@@ -270,7 +447,6 @@
     n_shot = lax.axis_size("shot")
     n_off = lax.axis_size("off")
     n_dev = n_shot * n_off
-    axes = ("shot", "off")
     tr_dev = shot_dev * tr_off
     rec_dev = rec_owner.shape[0] // n_shot
     cmp_dev = cmp_owner.shape[0] // n_shot
@@ -282,24 +458,17 @@
     local_ids = jnp.stack(
         [offset_bin.reshape(tr_dev), rec_id.reshape(tr_dev), cmp_id.reshape(tr_dev)]
     )
-    ids = lax.all_gather(local_ids, axes, axis=0)
-    blocks = log_blocks(traces.reshape(tr_dev, samples), n_dev, held, padded)
-    logs = lax.all_to_all(blocks, axes, split_axis=0, concat_axis=0, tiled=True)
+    logs, ids = log_blocks(
+        traces.reshape(tr_dev, samples), local_ids, n_off, n_dev, held, padded
+    )
     sizes = (n_shot, n_off, shot_dev, held, rec_dev, cmp_dev)
     wide = lambda table: table.reshape(-1, WIDE)
     terms = run_sweeps(
         logs, ids, wide(rec_owner), wide(rec_slot), wide(cmp_owner), wide(cmp_slot), sizes, columns
     )
-    parts = lax.all_to_all(terms, axes, split_axis=0, concat_axis=0, tiled=True)
-    held_rows = parts[:, :held].reshape(n_dev * held, columns)[:NF]
-    rows = held_rows.astype(jnp.float32).T
     base = rec_rows + cmp_rows
-    return (
-        rows[base + OFFB_DEV : base + OFFB_DEV + shot_dev],
-        rows[base : base + OFFB_DEV],
-        rows[:rec_rows],
-        rows[rec_rows:base],
-    )
+    splits = (rec_rows, base, base + OFFB_DEV, base + OFFB_DEV + shot_dev)
+    return return_terms(terms, n_off, splits)
 
 
 def solution(mesh):

time: 164 us -> 135 us (0.82)
  blocking collectives: 71.4 us -> 0 us
  Pallas kernels: 70.4 us -> 118 us
  starting transfers between devices: 7.33 us -> 0 us
  local copies, waits for them, and re-layouts: 7.61 us -> 13.5 us
  other arithmetic: 5.8 us -> 0.61 us
    all_gather x1 -> x0, blocking collectives: 55.6 us -> none  [shards(): ids = lax.all_gather(local_ids, axes, axis=0)]
    pallas_call x1 -> x2, Pallas kernels: 12.3 us -> 60.4 us  [the longest x1 46.8 us: log_blocks(): pl.pallas_call(lambda *refs: logs_kernel(n_off, groups, *refs), out_shape...]
    all_to_all x1 -> x0, blocking collectives: 15.8 us -> none  [shards(): parts = lax.all_to_all(terms, axes, split_axis=0, concat_axis=0, tiled=True)]
    all_to_all x1 -> x0, starting transfers between devices: 7.33 us -> none  [shards(): logs = lax.all_to_all(blocks, axes, split_axis=0, concat_axis=0, tiled=True)]
    sin x2 -> x0, other arithmetic: 4.78 us -> none  [the longest x1 2.6 us: base_angles(): jnp.sin(fine_angle)]
    reshape x4, local copies, waits for them, and re-layouts: 2.42 us -> 5.24 us  [shards(): wide = lambda table: table.reshape(-1, WIDE)]
    another operation x3, local copies, waits for them, and re-layouts: 0.25 us -> 2.31 us  [shards(): jnp.stack([offset_bin.reshape(tr_dev), rec_id.reshape(tr_dev), cmp_id.res...]
    unnamed x20 -> x4, local copies, waits for them, and re-layouts: 4.25 us -> 5.95 us
  transfers between devices with their start and end apart: 1 -> 0, of which waited for: 0 -> 0; matrix products, arithmetic and copies ran while one was open for 2% -> 0% of each run, Pallas kernels for 0% -> 0%
where the time goes in v2:
time: 135 us; the launch traced here: 133 us
  Pallas kernels  118 us (87%)
  local copies, waits for them, and re-layouts  13.5 us (10%)
    pallas_call x1, Pallas kernels, run_sweeps(): pl.pallas_call(lambda *refs: sweeps_kernel(sizes, *refs), out_shape=jax.S...  58.1 us
    pallas_call x1, Pallas kernels, log_blocks(): pl.pallas_call(lambda *refs: logs_kernel(n_off, groups, *refs), out_shape...  46.8 us
    pallas_call x1, Pallas kernels, return_terms(): pl.pallas_call(lambda *refs: return_kernel(n_off, splits, *refs), out_sha...  13.6 us
    unnamed x4, local copies, waits for them, and re-layouts  5.95 us
    reshape x4, local copies, waits for them, and re-layouts, shards(): wide = lambda table: table.reshape(-1, WIDE)  5.24 us

profile of v2, /device:TPU:0, one launch (start us, length us, event | category | flops | bytes accessed | tf_op | source)
XLA Modules:
  0.0 133.2 jit_solution(13896214377990538217)
XLA Ops:
  0.6 0.8 stack_reshape.9
  1.4 0.8 stack_reshape.10
  2.2 0.8 stack_reshape.11
  2.9 0.6 pad_add_fusion.refs_1_
  3.6 1.3 reshape.24.refs_2_
  4.9 1.3 reshape.25.refs_3_
  6.1 1.3 reshape.26.refs_4_
  7.5 1.3 reshape.27.refs_5_
  8.8 46.8 %logs.1 = (bf16[32,24,768]{2,1,0:T(8,128)(2,1)}, s32[32,3,768]{2,1,0:T(4,128)}) custom-call(bf16[768,2048]{1,0:T(8,128)(2,1)} %bitcast.1, s32[3,768]{1,0:T(4,128)} %pad_add_fusion.refs_1_, f32[768,16]{1,0:T(8,128)} %constant.10.clone.refs_2_, f32[768,16]{1,0:T(8,128)} %constant.11.clone.refs_3_, f32[768,128]{1,0:T(8,128)} %constant.12.clone.refs_4_, ...), custom_call_target="tpu_custom_call" | custom-call | tf_op jit(solution)/shard_map/logs/pallas_call | solution.py:176
  55.6 58.1 %sweeps.1.refs_0_ = bf16[32,24,256]{2,1,0:T(8,128)(2,1)} custom-call(bf16[32,24,768]{2,1,0:T(8,128)(2,1)} %get-tuple-element.6.refs_0_, s32[32,3,768]{2,1,0:T(4,128)} %get-tuple-element.7.refs_1_, s32[8,256]{1,0:T(8,128)} %reshape.24.refs_2_, s32[8,256]{1,0:T(8,128)} %reshape.25.refs_3_, s32[16,256]{1,0:T(8,128)} %reshape.26.refs_4_, s32[16,256]{1,0:T(8,128)} %reshape.27.refs_5_), custom_call_target="tpu_custom_call" | custom-call | tf_op jit(solution)/shard_map/sweeps/pallas_call | solution.py:424
  113.7 13.6 %returns.1 = (f32[4,640]{1,0:T(4,128)}, f32[8,640]{1,0:T(8,128)}, f32[64,640]{1,0:T(8,128)}, f32[128,640]{1,0:T(8,128)}) custom-call(bf16[32,24,256]{2,1,0:T(8,128)(2,1)} %sweeps.1.refs_0_), custom_call_target="tpu_custom_call" | custom-call | tf_op jit(solution)/shard_map/returns/pallas_call | solution.py:256
  127.3 1.3 copy.21
  128.6 1.3 %copy.22 = f32[8,640]{1,0:T(8,128)} copy(f32[8,640]{1,0:T(8,128)} %get-tuple-element.13) | data formatting | bytes 40960
  129.9 1.6 %copy.23 = f32[64,640]{1,0:T(8,128)} copy(f32[64,640]{1,0:T(8,128)} %get-tuple-element.14) | data formatting | bytes 327680
  131.5 1.7 %copy.24 = f32[128,640]{1,0:T(8,128)} copy(f32[128,640]{1,0:T(8,128)} %get-tuple-element.15) | data formatting | bytes 655360

commit v3 on v2

--- a/solution.py
+++ b/solution.py
@@ -74,48 +74,48 @@
     return barrier
 
 
-def logs_kernel(
-    n_off,
-    groups,
-    traces_ref,
-    ids_ref,
-    ca_ref,
-    sa_ref,
-    cb_ref,
-    sb_ref,
-    w_ref,
-    out_ref,
-    ids_out_ref,
-    stage,
-    table,
-    send_sems,
-    recv_sems,
-    id_send_sems,
-    id_recv_sems,
-    own_sems,
-):
-    n_dev, padded, tr_dev = out_ref.shape
+def send_logs(n_off, groups, held, traces_ref, id_refs, table_refs, landed, bins, scratch):
+    ca_ref, sa_ref, cb_ref, sb_ref, w_ref = table_refs
+    stage, own_bins, id_rows, table, send_sems, recv_sems, bin_send_sems, bin_recv_sems, own_sems = (
+        scratch
+    )
+    n_dev, padded, tr_dev = landed.shape
     dests = n_dev // groups
     rows = dests * padded
     me = my_position(n_off)
     barrier = greet_all(me, n_dev, n_off)
+    bin_ref, rec_ref, cmp_ref = id_refs
+    shot_dev, tr_off = bin_ref.shape
+    id_rows[...] = jnp.zeros_like(id_rows)
+    for shot in range(shot_dev):
+        cols = slice(shot * tr_off, (shot + 1) * tr_off)
+        own_bins[:, cols] = bin_ref[shot : shot + 1, :]
+        rec = rec_ref[shot : shot + 1, :]
+        cmp = cmp_ref[shot : shot + 1, :]
+        parts = (rec % WIDE, rec // WIDE, cmp % WIDE, cmp // WIDE)
+        for k, part in enumerate(parts):
+            id_rows[held + k : held + k + 1, cols] = part.astype(jnp.float32)
 
     def block_copy(dest, slot):
         return remote(
-            stage.at[dest], out_ref.at[slot], send_sems.at[dest], recv_sems.at[slot], dest, n_off
+            stage.at[dest], landed.at[slot], send_sems.at[dest], recv_sems.at[slot], dest, n_off
         )
 
-    def id_copy(dest, slot):
+    def bin_copy(dest, slot):
         return remote(
-            ids_ref, ids_out_ref.at[slot], id_send_sems.at[dest], id_recv_sems.at[slot], dest, n_off
+            own_bins, bins.at[slot], bin_send_sems.at[dest], bin_recv_sems.at[slot], dest, n_off
         )
 
-    own_ids = pltpu.make_async_copy(ids_ref, ids_out_ref.at[me], own_sems.at[0])
-    own_ids.start()
+    def turn_group(turn):
+        if groups & (groups - 1) == 0:
+            return (me // dests) ^ (groups - 1 - turn)
+        return ((me // dests) + groups - 1 - turn) % groups
+
+    own_copy = pltpu.make_async_copy(own_bins, bins.at[me], own_sems.at[0])
+    own_copy.start()
+    freq_row = lax.broadcasted_iota(jnp.int32, (dests, padded, tr_dev), 1)
     for turn in range(groups):
-        group = ((me // dests) + groups - 1 - turn) % groups
-        if groups & (groups - 1) == 0:
-            group = (me // dests) ^ (groups - 1 - turn)
+        group = turn_group(turn)
         base = pl.multiple_of(group * rows, 8)
         cb = cb_ref[pl.ds(base, rows), :]
         sb = sb_ref[pl.ds(base, rows), :]
@@ -132,9 +132,9 @@
         real_part = products[:rows]
         imag_part = products[rows:]
         logs = jnp.log(real_part * real_part + imag_part * imag_part + FLOOR)
-        stage[pl.ds(group * dests, dests)] = logs.astype(jnp.bfloat16).reshape(
-            dests, padded, tr_dev
-        )
+        logs = logs.reshape(dests, padded, tr_dev)
+        logs = jnp.where(freq_row < held, logs, id_rows[...][None])
+        stage[pl.ds(group * dests, dests)] = logs.astype(jnp.bfloat16)
         if turn == 0:
             pl.semaphore_wait(barrier, n_dev - 1)
 
@@ -145,56 +145,31 @@
             @pl.when(dest != me)
             def _():
                 block_copy(dest, me).start()
-
-        if turn == 0:
-
-            @pl.loop(1, n_dev)
-            def _(step):
-                id_copy((me + step) % n_dev, me).start()
-
-    own = pltpu.make_async_copy(stage.at[me], out_ref.at[me], own_sems.at[1])
+                bin_copy(dest, me).start()
+
+    own = pltpu.make_async_copy(stage.at[me], landed.at[me], own_sems.at[1])
     own.start()
-
-    @pl.loop(1, n_dev)
-    def _(step):
-        dest = (me + step) % n_dev
-        block_copy(dest, me).wait_send()
-        id_copy(dest, me).wait_send()
-        block_copy(dest, dest).wait_recv()
-        id_copy(dest, dest).wait_recv()
-
+    own_copy.wait()
     own.wait()
-    own_ids.wait()
-
-
-def log_blocks(traces, ids, n_off, n_dev, held, padded):
-    tr_dev, samples = traces.shape
-    groups = 4 if n_dev % 4 == 0 else 1
-    rows = n_dev // groups * padded
-    tables = base_angles(samples, n_dev, held, padded)
-    vmem = pl.BlockSpec(memory_space=pltpu.VMEM)
-    return pl.pallas_call(
-        lambda *refs: logs_kernel(n_off, groups, *refs),
-        out_shape=(
-            jax.ShapeDtypeStruct((n_dev, padded, tr_dev), jnp.bfloat16),
-            jax.ShapeDtypeStruct((n_dev,) + ids.shape, ids.dtype),
-        ),
-        in_specs=[vmem] * 7,
-        out_specs=(vmem, vmem),
-        scratch_shapes=[
-            pltpu.VMEM((n_dev, padded, tr_dev), jnp.bfloat16),
-            pltpu.VMEM((2 * rows, samples), jnp.bfloat16),
-            pltpu.SemaphoreType.DMA((n_dev,)),
-            pltpu.SemaphoreType.DMA((n_dev,)),
-            pltpu.SemaphoreType.DMA((n_dev,)),
-            pltpu.SemaphoreType.DMA((n_dev,)),
-            pltpu.SemaphoreType.DMA((2,)),
-        ],
-        compiler_params=pltpu.CompilerParams(
-            vmem_limit_bytes=VMEM_BYTES, collective_id=0, has_side_effects=True
-        ),
-        name="logs",
-    )(traces, ids, *tables)
+
+    def arrival(turn, step):
+        src = turn_group(turn) * dests + (me + dests - step) % dests
+
+        @pl.when(src != me)
+        def _():
+            block_copy(src, src).wait_recv()
+            bin_copy(src, src).wait_recv()
+
+        return src
+
+    def finish():
+        @pl.loop(1, n_dev)
+        def _(step):
+            dest = (me + step) % n_dev
+            block_copy(dest, me).wait_send()
+            bin_copy(dest, me).wait_send()
+
+    return arrival, finish
 
 
 def return_kernel(
@@ -274,12 +249,12 @@
 
 def one_hot(index, count):
     rows = lax.broadcasted_iota(jnp.int32, (count, index.shape[1]), 0)
-    return jnp.where(rows == index, 1.0, 0.0).astype(jnp.bfloat16)
+    return jnp.where(rows.astype(index.dtype) == index, 1.0, 0.0).astype(jnp.bfloat16)
 
 
 def level_mask(index, levels, rows):
     level = lax.broadcasted_iota(jnp.int32, (levels, rows, index.shape[1]), 0)
-    return level == index[None]
+    return level.astype(index.dtype) == index[None]
 
 
 def spread(values, mask):
@@ -295,13 +270,22 @@
 
 def sweeps_kernel(
     sizes,
-    logs_ref,
-    ids_ref,
+    traces_ref,
+    bin_ref,
+    rec_ref,
+    cmp_ref,
+    ca_ref,
+    sa_ref,
+    cb_ref,
+    sb_ref,
+    w_ref,
     rec_owner_ref,
     rec_slot_ref,
     cmp_owner_ref,
     cmp_slot_ref,
     out_ref,
+    landed,
+    bins,
     rec_acc,
     cmp_acc,
     so_acc,
@@ -311,9 +295,12 @@
     rec_b,
     cmp_b,
     placed,
+    *send_scratch,
 ):
     n_shot, n_off, shot_dev, held, rec_dev, cmp_dev = sizes
-    n_dev, padded, tr_dev = logs_ref.shape
+    n_dev, padded, tr_dev = landed.shape
+    groups = 4 if n_dev % 4 == 0 else 1
+    dests = n_dev // groups
     tr_off = tr_dev // shot_dev
     n_bins = n_off * OFFB_DEV
     rec_l = rec_acc.shape[0] // padded
@@ -321,40 +308,59 @@
     so_width = so_acc.shape[1]
     freq_row = lax.broadcasted_iota(jnp.int32, (padded, tr_dev), 0)
     local_shot = lax.broadcasted_iota(jnp.int32, (1, tr_dev), 1) // tr_off
+    arrival, finish = send_logs(
+        n_off,
+        groups,
+        held,
+        traces_ref,
+        (bin_ref, rec_ref, cmp_ref),
+        (ca_ref, sa_ref, cb_ref, sb_ref, w_ref),
+        landed,
+        bins,
+        send_scratch,
+    )
+
+    def add_source(src, first):
+        values = landed[src].astype(jnp.float32)
+        rec_h, rec_level, cmp_h, cmp_level = (
+            values[held + k : held + k + 1] for k in range(4)
+        )
+        shot = (src // n_off) * shot_dev + local_shot + n_bins
+        so_row = lax.broadcasted_iota(jnp.int32, (so_width, tr_dev), 0)
+        so_hot = jnp.where((so_row == bins[src]) | (so_row == shot), 1.0, 0.0).astype(jnp.bfloat16)
+        rec_hot = one_hot(rec_h, WIDE)
+        cmp_hot = one_hot(cmp_h, WIDE)
+        rec_mask = level_mask(rec_level, rec_l, padded)
+        cmp_mask = level_mask(cmp_level, cmp_l, padded)
+        if first:
+            values = jnp.where(freq_row == held, 1.0, values)
+        else:
+            so_part = dot_nn(so_x[...], so_hot)
+            rec_part = dot_nn(rec_x[...], rec_hot).reshape(rec_mask.shape)
+            cmp_part = dot_nn(cmp_x[...], cmp_hot).reshape(cmp_mask.shape)
+            values = values - (so_part[:padded] + so_part[padded:])
+            values = values - jnp.sum(jnp.where(rec_mask, rec_part, 0.0), axis=0)
+            values = values - jnp.sum(jnp.where(cmp_mask, cmp_part, 0.0), axis=0)
+        rec_acc[...] += dot_nt(spread(values, rec_mask), rec_hot)
+        cmp_acc[...] += dot_nt(spread(values, cmp_mask), cmp_hot)
+        so_acc[...] += dot_nt(values.astype(jnp.bfloat16), so_hot)
 
     def sums_over_traces(first):
         rec_acc[...] = jnp.zeros_like(rec_acc)
         cmp_acc[...] = jnp.zeros_like(cmp_acc)
         so_acc[...] = jnp.zeros_like(so_acc)
-
+        if not first:
+
+            @pl.loop(0, n_dev)
+            def _(src):
+                add_source(src, False)
+
+            return
         @pl.loop(0, n_dev)
-        def _(src):
-            ids = ids_ref[src]
-            rec = ids[1:2]
-            cmp = ids[2:3]
-            shot = (src // n_off) * shot_dev + local_shot + n_bins
-            so_row = lax.broadcasted_iota(jnp.int32, (so_width, tr_dev), 0)
-            so_hot = jnp.where((so_row == ids[0:1]) | (so_row == shot), 1.0, 0.0).astype(
-                jnp.bfloat16
-            )
-            rec_hot = one_hot(rec % WIDE, WIDE)
-            cmp_hot = one_hot(cmp % WIDE, WIDE)
-            rec_mask = level_mask(rec // WIDE, rec_l, padded)
-            cmp_mask = level_mask(cmp // WIDE, cmp_l, padded)
-            values = logs_ref[src].astype(jnp.float32)
-            if first:
-                values = jnp.where(freq_row == held, 1.0, values)
-            else:
-                so_part = dot_nn(so_x[...], so_hot)
-                rec_part = dot_nn(rec_x[...], rec_hot).reshape(rec_mask.shape)
-                cmp_part = dot_nn(cmp_x[...], cmp_hot).reshape(cmp_mask.shape)
-                values = values - (so_part[:padded] + so_part[padded:])
-                values = values - jnp.sum(jnp.where(rec_mask, rec_part, 0.0), axis=0)
-                values = values - jnp.sum(jnp.where(cmp_mask, cmp_part, 0.0), axis=0)
-            rec_acc[...] += dot_nt(spread(values, rec_mask), rec_hot)
-            cmp_acc[...] += dot_nt(spread(values, cmp_mask), cmp_hot)
-            so_sums = dot_nt(split_float(values), so_hot)
-            so_acc[...] += so_sums[:padded] + so_sums[padded:]
+        def _(step):
+            add_source(arrival(step // dests, step % dests), True)
+
+        finish()
 
     def update(sums, counts, levels):
         shaped = sums.reshape(levels, padded, sums.shape[1])
@@ -391,13 +397,15 @@
 
     @pl.loop(0, rec_l)
     def _(level):
-        position = rec_owner_ref[pl.ds(level, 1)] * rec_dev + rec_slot_ref[pl.ds(level, 1)]
+        span = pl.ds(pl.multiple_of(level * WIDE, WIDE), WIDE)
+        position = (rec_owner_ref[span] * rec_dev + rec_slot_ref[span]).reshape(1, WIDE)
         values = rec_acc[pl.ds(pl.multiple_of(level * padded, 8), padded), :]
         place(values, position // rec_rows, position % rec_rows)
 
     @pl.loop(0, cmp_l)
     def _(level):
-        position = cmp_owner_ref[pl.ds(level, 1)] * cmp_dev + cmp_slot_ref[pl.ds(level, 1)]
+        span = pl.ds(pl.multiple_of(level * WIDE, WIDE), WIDE)
+        position = (cmp_owner_ref[span] * cmp_dev + cmp_slot_ref[span]).reshape(1, WIDE)
         values = cmp_acc[pl.ds(pl.multiple_of(level * padded, 8), padded), :]
         place(values, position // cmp_rows, position % cmp_rows + rec_rows)
 
@@ -415,18 +423,25 @@
     out_ref[...] = placed[...].astype(jnp.bfloat16).reshape(out_ref.shape)
 
 
-def run_sweeps(logs, ids, rec_owner, rec_slot, cmp_owner, cmp_slot, sizes, columns):
-    n_shot, n_off, shot_dev, _, _, _ = sizes
-    n_dev, padded, _ = logs.shape
-    rec_l = rec_owner.shape[0]
-    cmp_l = cmp_owner.shape[0]
+def run_sweeps(traces, ids, owners, sizes, padded, columns):
+    n_shot, n_off, shot_dev, held, _, _ = sizes
+    n_dev = n_shot * n_off
+    tr_dev, samples = traces.shape
+    groups = 4 if n_dev % 4 == 0 else 1
+    rows = n_dev // groups * padded
+    rec_l = owners[0].shape[0] // WIDE
+    cmp_l = owners[2].shape[0] // WIDE
     so_width = up(n_shot * shot_dev + n_off * OFFB_DEV, LANES)
+    tables = base_angles(samples, n_dev, held, padded)
+    vmem = pl.BlockSpec(memory_space=pltpu.VMEM)
     return pl.pallas_call(
         lambda *refs: sweeps_kernel(sizes, *refs),
         out_shape=jax.ShapeDtypeStruct((n_dev, padded, columns), jnp.bfloat16),
-        in_specs=[pl.BlockSpec(memory_space=pltpu.VMEM)] * 6,
-        out_specs=pl.BlockSpec(memory_space=pltpu.VMEM),
+        in_specs=[vmem] * 13,
+        out_specs=vmem,
         scratch_shapes=[
+            pltpu.VMEM((n_dev, padded, tr_dev), jnp.bfloat16),
+            pltpu.VMEM((n_dev, 1, tr_dev), jnp.int32),
             pltpu.VMEM((rec_l * padded, WIDE), jnp.float32),
             pltpu.VMEM((cmp_l * padded, WIDE), jnp.float32),
             pltpu.VMEM((padded, so_width), jnp.float32),
@@ -436,10 +451,21 @@
             pltpu.VMEM((rec_l * padded, WIDE), jnp.float32),
             pltpu.VMEM((cmp_l * padded, WIDE), jnp.float32),
             pltpu.VMEM((n_dev * padded, columns), jnp.float32),
+            pltpu.VMEM((n_dev, padded, tr_dev), jnp.bfloat16),
+            pltpu.VMEM((1, tr_dev), jnp.int32),
+            pltpu.VMEM((padded, tr_dev), jnp.float32),
+            pltpu.VMEM((2 * rows, samples), jnp.bfloat16),
+            pltpu.SemaphoreType.DMA((n_dev,)),
+            pltpu.SemaphoreType.DMA((n_dev,)),
+            pltpu.SemaphoreType.DMA((n_dev,)),
+            pltpu.SemaphoreType.DMA((n_dev,)),
+            pltpu.SemaphoreType.DMA((2,)),
         ],
-        compiler_params=pltpu.CompilerParams(vmem_limit_bytes=VMEM_BYTES),
+        compiler_params=pltpu.CompilerParams(
+            vmem_limit_bytes=VMEM_BYTES, collective_id=0, has_side_effects=True
+        ),
         name="sweeps",
-    )(logs, ids, rec_owner, rec_slot, cmp_owner, cmp_slot)
+    )(traces, *ids, *tables, *owners)
 
 
 def shards(traces, offset_bin, rec_id, cmp_id, rec_owner, rec_slot, cmp_owner, cmp_slot):
@@ -453,18 +479,15 @@
     rec_rows = rec_dev // n_off
     cmp_rows = cmp_dev // n_off
     held = up(NF, n_dev) // n_dev
-    padded = up(held + 1, 8)
+    padded = up(held + 4, 8)
     columns = up(rec_rows + cmp_rows + shot_dev + OFFB_DEV, LANES)
-    local_ids = jnp.stack(
-        [offset_bin.reshape(tr_dev), rec_id.reshape(tr_dev), cmp_id.reshape(tr_dev)]
-    )
-    logs, ids = log_blocks(
-        traces.reshape(tr_dev, samples), local_ids, n_off, n_dev, held, padded
-    )
-    sizes = (n_shot, n_off, shot_dev, held, rec_dev, cmp_dev)
-    wide = lambda table: table.reshape(-1, WIDE)
     terms = run_sweeps(
-        logs, ids, wide(rec_owner), wide(rec_slot), wide(cmp_owner), wide(cmp_slot), sizes, columns
+        traces.reshape(tr_dev, samples),
+        (offset_bin, rec_id, cmp_id),
+        (rec_owner, rec_slot, cmp_owner, cmp_slot),
+        (n_shot, n_off, shot_dev, held, rec_dev, cmp_dev),
+        padded,
+        columns,
     )
     base = rec_rows + cmp_rows
     splits = (rec_rows, base, base + OFFB_DEV, base + OFFB_DEV + shot_dev)

time: 135 us -> 109 us (0.81)
  Pallas kernels: 118 us -> 101 us
  local copies, waits for them, and re-layouts: 13.5 us -> 5.95 us
    pallas_call x1 -> x0, Pallas kernels: 46.8 us -> none  [log_blocks(): pl.pallas_call(lambda *refs: logs_kernel(n_off, groups, *refs), out_shape...]
    pallas_call x1, Pallas kernels: 58.1 us -> 88 us  [run_sweeps(): pl.pallas_call(lambda *refs: sweeps_kernel(sizes, *refs), out_shape=jax.S...]
    reshape x4 -> x0, local copies, waits for them, and re-layouts: 5.24 us -> none  [shards(): wide = lambda table: table.reshape(-1, WIDE)]
    another operation x3 -> x0, local copies, waits for them, and re-layouts: 2.31 us -> none  [shards(): jnp.stack([offset_bin.reshape(tr_dev), rec_id.reshape(tr_dev), cmp_id.res...]
where the time goes in v3:
time: 109 us; the launch traced here: 108 us
  Pallas kernels  101 us (93%)
  local copies, waits for them, and re-layouts  5.95 us (5%)
    pallas_call x1, Pallas kernels, run_sweeps(): pl.pallas_call(lambda *refs: sweeps_kernel(sizes, *refs), out_shape=jax.S...  88 us
    pallas_call x1, Pallas kernels, return_terms(): pl.pallas_call(lambda *refs: return_kernel(n_off, splits, *refs), out_sha...  13.1 us
    unnamed x4, local copies, waits for them, and re-layouts  5.95 us

profile of v3, /device:TPU:0, one launch (start us, length us, event | category | flops | bytes accessed | tf_op | source)
XLA Modules:
  0.0 107.8 jit_solution(7108909261788641729)
XLA Ops:
  0.6 88.0 %sweeps.1.refs_0_ = bf16[32,24,256]{2,1,0:T(8,128)(2,1)} custom-call(bf16[768,2048]{1,0:T(8,128)(2,1)} %bitcast.1, s32[4,192]{1,0:T(4,128)} %refs_1_.1, s32[4,192]{1,0:T(4,128)} %refs_2_.1, s32[4,192]{1,0:T(4,128)} %refs_3_.1, f32[768,16]{1,0:T(8,128)} %constant.10.clone.refs_4_, f32[768,16]{1,0:T(8,128)} %constant.11.clone.refs_5_, ...), custom_call_target="tpu_custom_call" | custom-call | tf_op jit(solution)/shard_map/sweeps/pallas_call | solution.py:437
  88.7 13.1 %returns.1 = (f32[4,640]{1,0:T(4,128)}, f32[8,640]{1,0:T(8,128)}, f32[64,640]{1,0:T(8,128)}, f32[128,640]{1,0:T(8,128)}) custom-call(bf16[32,24,256]{2,1,0:T(8,128)(2,1)} %sweeps.1.refs_0_), custom_call_target="tpu_custom_call" | custom-call | tf_op jit(solution)/shard_map/returns/pallas_call | solution.py:231
  101.8 1.3 %copy.21 = f32[4,640]{1,0:T(4,128)} copy(f32[4,640]{1,0:T(4,128)} %get-tuple-element.8) | data formatting | bytes 20480
  103.1 1.3 %copy.22 = f32[8,640]{1,0:T(8,128)} copy(f32[8,640]{1,0:T(8,128)} %get-tuple-element.9) | data formatting | bytes 40960
  104.4 1.6 %copy.23 = f32[64,640]{1,0:T(8,128)} copy(f32[64,640]{1,0:T(8,128)} %get-tuple-element.10) | data formatting | bytes 327680
  106.0 1.7 %copy.24 = f32[128,640]{1,0:T(8,128)} copy(f32[128,640]{1,0:T(8,128)} %get-tuple-element.11) | data formatting | bytes 655360
